TPU v7x, 32 devices: a whole 2x2x4 slice. The times are simulated.
32 devices in a mesh: role: 2 (over core), seq: 4 (over z), tp: 4 (over y, x).
Axes of the slice: x: 2, y: 2, z: 4, core: 2. Of those that a mesh axis runs over, the one named last changes fastest.
Arguments:
- merger_hidden: bfloat16 [512, 5120], P(('role', 'seq'), 'tp'), may hold values from -6 to 6
- merger_out: bfloat16 [5120, 8192], P('tp', ('role', 'seq')), may hold values from -0.078125 to 0.078125
- row_position: int32 [512], P(('role', 'seq')), may hold values from -1 to 2047, as said below
- prompt_embeds: bfloat16 [2048, 8192], P(('role', 'seq'), 'tp'), may hold values from -300 to 300
- norm_gain: bfloat16 [8192], P('tp'), may hold values from 0.099609375 to 1.8984375
- query_weight: bfloat16 [8192, 4096], P(None, 'tp'), may hold values from -2.762136 to 2.762136
- key_weight: bfloat16 [8192, 512], P(None, 'tp'), may hold values from -0.06629126 to 0.06629126
- value_weight: bfloat16 [8192, 512], P(None, 'tp'), may hold values from -0.0625 to 0.0625
Outputs:
- stream: bfloat16 [2048, 8192], P(('role', 'seq'), 'tp')
- context: bfloat16 [2048, 4096], P(('role', 'seq'), 'tp')
Inputs may be any that keep to these rules, and one draw needn't show every extreme that they name: `row_position`: the live slots of each device's 64 come first and hold distinct prompt positions, distinct over all devices; the other slots hold -1. Of one device's slots at most 16 hold positions of one owner's block (positions j * 256 to (j + 1) * 256 - 1); every device has 16 or more live slots.
All inputs are finite; a program needn't handle non-finite values.
Results may differ from a plain program's by a relative error of at most 0.012.
The roundings to bfloat16 on the way count: a program that leaves them out, or rounds other values in their place, can miss the bound.
Values may be sent and summed in bfloat16 or wider, within the bound.
No kernel may reach another device: no remote copies, remote signals or barrier semaphores. Data moves between devices by JAX's collectives and lax.ppermute only.
A program may use at most 192 MiB of HBM per device.

v0:
```python
import math
import jax
import jax.numpy as jnp
from jax import lax
from jax.sharding import PartitionSpec as P

HEAD_DIM = 128


def rotate(vectors, positions):
    half_dim = vectors.shape[-1] // 2
    frequency = 1000000.0 ** (-jnp.arange(half_dim, dtype=jnp.float32) / half_dim)
    angles = positions.astype(jnp.float32)[:, None, None] * frequency[None, None, :]
    cosine = jnp.cos(angles)
    sine_part = jnp.sin(angles)
    lower_half = vectors[..., :half_dim]
    upper_half = vectors[..., half_dim:]
    return jnp.concatenate(
        [
            lower_half * cosine - upper_half * sine_part,
            upper_half * cosine + lower_half * sine_part,
        ],
        axis=-1,
    )


def sum_hidden(partial_value):
    return lax.psum_scatter(partial_value, "tp", scatter_dimension=1, tiled=True).astype(
        jnp.bfloat16
    )


def project_strips(merger_hidden, merger_out):
    return jnp.dot(
        lax.all_gather(merger_hidden, ("role", "seq"), axis=0, tiled=True),
        merger_out,
        preferred_element_type=jnp.float32,
    )


def body(
    merger_hidden,
    merger_out,
    row_position,
    prompt_embeds,
    norm_gain,
    query_weight,
    key_weight,
    value_weight,
):
    groups = lax.axis_size("role") * lax.axis_size("seq")
    device_rank = lax.axis_index(("role", "seq"))
    row_count = merger_hidden.shape[0]
    tok_count = prompt_embeds.shape[0]
    columns = prompt_embeds.shape[1]
    model_width = columns * lax.axis_size("tp")
    capacity = 2 * row_count // groups
    strips = project_strips(merger_hidden, merger_out)
    partial_value = lax.all_to_all(strips, ("role", "seq"), split_axis=0, concat_axis=1, tiled=True)
    embeds = sum_hidden(partial_value)
    owners = jnp.where(row_position >= 0, row_position // tok_count, groups)
    onehot = (owners[:, None] == jnp.arange(groups, dtype=jnp.int32)[None, :]).astype(jnp.int32)
    earlier = jnp.sum((jnp.cumsum(onehot, axis=0) - onehot) * onehot, axis=1)
    buffer_slot = jnp.where(owners < groups, owners * capacity + earlier, groups * capacity)
    source = (
        jnp.full((groups * capacity,), row_count, jnp.int32)
        .at[buffer_slot]
        .set(jnp.arange(row_count, dtype=jnp.int32), mode="drop")
    )
    padded = jnp.concatenate([embeds, jnp.zeros((1, columns), jnp.bfloat16)], axis=0)
    outgoing = padded[source].reshape(groups, capacity, columns)
    outgoing_pos = jnp.concatenate([row_position, jnp.full((1,), -1, jnp.int32)])[source].reshape(
        groups, capacity
    )
    arrived, arrived_pos = (
        lax.all_to_all(outgoing, ("role", "seq"), split_axis=0, concat_axis=0, tiled=True),
        lax.all_to_all(outgoing_pos, ("role", "seq"), split_axis=0, concat_axis=0, tiled=True),
    )
    arrived_pos = arrived_pos.reshape(-1)
    local_row = jnp.where(arrived_pos >= 0, arrived_pos - device_rank * tok_count, tok_count)
    stream = prompt_embeds.at[local_row].set(arrived.reshape(-1, columns), mode="drop")
    widened = stream.astype(jnp.float32)
    squares = lax.psum(jnp.sum(widened * widened, axis=1), "tp")
    inverse = lax.rsqrt(squares / model_width + 1e-06)[:, None]
    normed = (widened * inverse * norm_gain.astype(jnp.float32)[None, :]).astype(jnp.bfloat16)
    tables = (query_weight, key_weight, value_weight)
    shard_piece = lax.all_gather(normed, "tp", axis=1, tiled=True)
    query_sum, key_sum, value_sum = tuple(
        (jnp.dot(shard_piece, table, preferred_element_type=jnp.float32) for table in tables)
    )
    local_heads = query_weight.shape[1] // HEAD_DIM
    local_kv = key_weight.shape[1] // HEAD_DIM
    group_size = local_heads // local_kv
    positions = device_rank * tok_count + jnp.arange(tok_count, dtype=jnp.int32)
    queries = rotate(query_sum.reshape(tok_count, local_heads, HEAD_DIM), positions).astype(
        jnp.bfloat16
    )
    queries = queries.reshape(tok_count, local_kv, group_size, HEAD_DIM)
    key_rows = rotate(key_sum.reshape(tok_count, local_kv, HEAD_DIM), positions).astype(
        jnp.bfloat16
    )
    value_rows = value_sum.astype(jnp.bfloat16).reshape(tok_count, local_kv, HEAD_DIM)
    score_scale = 1.0 / math.sqrt(HEAD_DIM)
    running_max = jnp.full((local_kv, group_size, tok_count), -1e30, jnp.float32)
    key_piece = lax.all_gather(key_rows, ("role", "seq"), axis=0, tiled=True)
    value_piece = lax.all_gather(value_rows, ("role", "seq"), axis=0, tiled=True)
    scores = (
        jnp.einsum("qhgd,khd->hgqk", queries, key_piece, preferred_element_type=jnp.float32)
        * score_scale
    )
    key_pos = jnp.arange(key_piece.shape[0], dtype=jnp.int32)
    visible = key_pos[None, :] <= positions[:, None]
    scores = jnp.where(visible, scores, -jnp.inf)
    next_max = jnp.maximum(running_max, jnp.max(scores, axis=3))
    probability = jnp.where(visible, jnp.exp(scores - next_max[..., None]), 0.0)
    running_sum = jnp.sum(probability, axis=3)
    running_out = jnp.einsum(
        "hgqk,khd->hgqd",
        probability.astype(jnp.bfloat16),
        value_piece,
        preferred_element_type=jnp.float32,
    )
    running_max, running_sum, running_out = (next_max, running_sum, running_out)
    context = running_out / running_sum[..., None]
    context = (
        jnp.transpose(context, (2, 0, 1, 3))
        .reshape(tok_count, local_heads * HEAD_DIM)
        .astype(jnp.bfloat16)
    )
    return (stream, context)


def solution(mesh):
    in_specs = (
        P(("role", "seq"), "tp"),
        P("tp", ("role", "seq")),
        P(("role", "seq")),
        P(("role", "seq"), "tp"),
        P("tp"),
        P(None, "tp"),
        P(None, "tp"),
        P(None, "tp"),
    )
    out_specs = (P(("role", "seq"), "tp"), P(("role", "seq"), "tp"))
    return jax.shard_map(body, mesh=mesh, in_specs=in_specs, out_specs=out_specs, check_vma=False)
```

profile of v0, /device:TPU:0, one launch (start us, length us, event | category | flops | bytes accessed | tf_op | source)
XLA Modules:
  0.0 304.1 jit_solution(15773914192989135023)
XLA Ops:
  7.2 2.5 copy.45
  9.8 26.2 %all-gather.4.cloned.1.call-done = bf16[512,1280]{1,0:T(8,128)(2,1)} async-done(((bf16[64,1280]{1,0:T(8,128)(2,1)}), bf16[512,1280]{1,0:T(8,128)(2,1)}) %all-gather.4.cloned.1.call-update) | async-done | bytes 1310736 | tf_op jit(solution)/shard_map/all_gather | solution.py:35
  36.0 2.8 fusion.37
  38.8 51.7 %all_to_all.33 = f32[8,64,1024]{2,1,0:T(8,128)S(1)} all-to-all(f32[8,64,1024]{2,1,0:T(8,128)S(1)} %bitcast.65), channel_id=1, replica_groups=mesh['role'=2,'seq'=4,'tp'=4] {'role','seq'}, dimensions={0} | all-to-all | bytes 4194304 | tf_op jit(solution)/shard_map/all_to_all | solution.py:59
  90.5 1.5 copy.37
  95.2 3.3 %all-to-all-start = ((s32[8,1,16]{2,1,0:T(1,128)}), s32[8,1,16]{2,1,0:T(1,128)S(1)}, u32[]{:S(2)}, u32[]{:S(2)}) async-start(s32[8,1,16]{2,1,0:T(1,128)} %bitcast), calls=%async_computation | async-start | bytes 8192 | tf_op jit(solution)/shard_map/all_to_all | solution.py:77
  98.5 27.3 %reduce-scatter.2.cloned.1.call-done = f32[64,2048]{1,0:T(8,128)} async-done(((f32[64,8192]{1,0:T(8,128)}), f32[64,2048]{1,0:T(8,128)}) %reduce-scatter.2.cloned.1.call-update) | async-done | bytes 524304 | tf_op jit(solution)/shard_map/reduce_scatter | solution.py:28
  127.0 1.7 gather_fusion.1
  128.7 4.6 %all-to-all-start.2 = ((bf16[8,16,2048]{2,1,0:T(8,128)(2,1)}), bf16[8,16,2048]{2,1,0:T(8,128)(2,1)S(1)}, u32[]{:S(2)}, u32[]{:S(2)}) async-start(bf16[8,16,2048]{2,1,0:T(8,128)(2,1)} %bitcast.4), calls=%async_computation.3 | async-start | bytes 1048576 | tf_op jit(solution)/shard_map/all_to_all | solution.py:76
  133.5 14.6 %all-to-all-done.2 = bf16[8,16,2048]{2,1,0:T(8,128)(2,1)S(1)} async-done(((bf16[8,16,2048]{2,1,0:T(8,128)(2,1)}), bf16[8,16,2048]{2,1,0:T(8,128)(2,1)S(1)}, u32[]{:S(2)}, u32[]{:S(2)}) %all-to-all-start.2) | async-done | bytes 524320 | tf_op jit(solution)/shard_map/all_to_all | solution.py:76
  148.0 3.7 %scatter_fusion = bf16[256,2048]{1,0:T(8,128)(2,1)} fusion(bf16[256,2048]{1,0:T(8,128)(2,1)} %copy.45, s32[128]{0:T(128)S(1)} %fusion.28, bf16[128,2048]{1,0:T(8,128)(2,1)S(1)} %bitcast.64), kind=kCustom, calls=%fused_computation.3 | custom fusion | bytes 1573376 | tf_op jit(solution)/shard_map/scatter | solution.py:81
  151.7 1.5 fusion.7
  153.2 8.9 %psum.7 = f32[256]{0:T(256)S(1)} all-reduce(f32[256]{0:T(256)S(1)} %fusion.7), channel_id=1, replica_groups=mesh['role'=2,'seq'=4,'tp'=4] {'tp'}, use_global_device_ids=true, to_apply=%region_6.7 | all-reduce | flops 256 | bytes 2048 | tf_op jit(solution)/shard_map/psum | solution.py:83
  162.2 2.5 fusion.9
  165.6 49.5 %all-gather.6.cloned.1.call-done = bf16[256,8192]{1,0:T(8,128)(2,1)} async-done(((bf16[256,2048]{1,0:T(8,128)(2,1)}), bf16[256,8192]{1,0:T(8,128)(2,1)}) %all-gather.6.cloned.1.call-update) | async-done | bytes 4194320 | tf_op jit(solution)/shard_map/all_gather | solution.py:87
  215.1 4.5 %convolution_bitcast_fusion.1 = f32[256,1,128]{0,2,1:T(8,128)S(1)} fusion(bf16[256,8192]{1,0:T(8,128)(2,1)} %all-gather.6.cloned.1.call-done, bf16[8192,128]{1,0:T(8,128)(2,1)} %param.14), kind=kOutput, calls=%fused_computation.19 | convolution fusion | flops 536870912 | bytes 6422528 | tf_op jit(solution)/shard_map/dot_general | solution.py:89
  219.9 8.4 %convolution_bitcast_fusion = f32[32,8,8,128]{3,1,2,0:T(8,128)S(1)} fusion(bf16[256,8192]{1,0:T(8,128)(2,1)S(1)} %copy-done.1, bf16[8192,1024]{1,0:T(8,128)(2,1)} %param.13), kind=kOutput, calls=%fused_computation.18 | convolution fusion | flops 4294967296 | bytes 22020096 | tf_op jit(solution)/shard_map/dot_general | solution.py:89
  228.6 26.5 %all_gather.14 = bf16[2048,1,128]{0,2,1:T(8,128)(2,1)S(1)} all-gather(bf16[256,1,128]{0,2,1:T(8,128)(2,1)S(1)} %pad_maximum_fusion), channel_id=1, replica_groups=mesh['role'=2,'seq'=4,'tp'=4] {'role','seq'}, dimensions={0}, use_global_device_ids=true | all-gather | bytes 589824 | tf_op jit(solution)/shard_map/all_gather | solution.py:105
  255.1 1.2 convolution_convert_fusion
  256.3 26.6 %all-gather = bf16[2048,128]{1,0:T(8,128)(2,1)S(1)} all-gather(bf16[256,128]{1,0:T(8,128)(2,1)S(1)} %convolution_convert_fusion), channel_id=2, replica_groups=mesh['role'=2,'seq'=4,'tp'=4] {'role','seq'}, dimensions={0}, use_global_device_ids=true | all-gather | bytes 589824 | tf_op jit(solution)/shard_map/all_gather | solution.py:106
  283.7 2.8 fusion
  286.6 4.0 %fusion.1 = f32[8,256]{1,0:T(8,128)S(1)} fusion(f32[2048,256,8]{1,0,2:T(8,128)S(1)} %get-tuple-element.17, f32[8,256]{1,0:T(8,128)S(1)} %broadcast_maximum_fusion, pred[256,2048]{0,1:T(8,128)(4,1)S(1)} %iota_compare_fusion), kind=kLoop, calls=%fused_computation.7 | loop fusion | flops 20969472 | bytes 17317888 | tf_op jit(solution)/shard_map/reduce_sum | solution.py:116
  290.6 4.9 %divide_convert_fusion = bf16[8,256,128]{1,2,0:T(8,128)(2,1)} fusion(f32[2048,256,8]{1,0,2:T(8,128)S(1)} %get-tuple-element.17, f32[8,256]{1,0:T(8,128)S(1)} %broadcast_maximum_fusion, pred[256,2048]{0,1:T(8,128)(4,1)S(1)} %iota_compare_fusion, bf16[2048,128]{1,0:T(8,128)(2,1)S(1)} %all-gather, f32[8,256]{1,0:T(8,128)S(1)} %fusion.1), kind=kOutput, calls=%fused_computation.21 | convolution fusion | flops 1095237632 | bytes 18366464 | tf_op jit(solution)/shard_map/hgqk,khd->hgqd/dot_general | solution.py:117
  295.5 2.0 copy.29
  (47 shorter events, 6.7 us)
Async XLA Ops:
  7.2 28.8 %copy-start = (bf16[1280,1024]{1,0:T(8,128)(2,1)S(1)}, bf16[1280,1024]{1,0:T(8,128)(2,1)}, u32[]{:S(2)}) copy-start(bf16[1280,1024]{1,0:T(8,128)(2,1)} %param.9) | copy-start | bytes 7864324
  7.2 28.8 %all-gather.4.cloned.1.call-start = ((), (), s32[]{:S(2)}) async-start(), calls=%async_computation.4 | async-start | bytes 1474560 | tf_op jit(solution)/shard_map/all_gather | solution.py:35
  9.7 116.1 %reduce-scatter.2.cloned.1.call-start = ((), (), s32[]{:S(2)}) async-start(), calls=%async_computation.5 | async-start | bytes 2621440 | tf_op jit(solution)/shard_map/reduce_scatter | solution.py:28
  90.5 1.5 copy-start.4
  92.1 41.3 %copy-start.3 = (bf16[2048]{0:T(1024)(128)(2,1)S(1)}, bf16[2048]{0:T(1024)(128)(2,1)}, u32[]{:S(2)}) copy-start(bf16[2048]{0:T(1024)(128)(2,1)} %param.12) | copy-start | bytes 12292
  95.2 33.4 %all-to-all-start = ((s32[8,1,16]{2,1,0:T(1,128)}), s32[8,1,16]{2,1,0:T(1,128)S(1)}, u32[]{:S(2)}, u32[]{:S(2)}) async-start(s32[8,1,16]{2,1,0:T(1,128)} %bitcast), calls=%async_computation | async-start | bytes 8192 | tf_op jit(solution)/shard_map/all_to_all | solution.py:77
  128.7 19.4 %all-to-all-start.2 = ((bf16[8,16,2048]{2,1,0:T(8,128)(2,1)}), bf16[8,16,2048]{2,1,0:T(8,128)(2,1)S(1)}, u32[]{:S(2)}, u32[]{:S(2)}) async-start(bf16[8,16,2048]{2,1,0:T(8,128)(2,1)} %bitcast.4), calls=%async_computation.3 | async-start | bytes 1048576 | tf_op jit(solution)/shard_map/all_to_all | solution.py:76
  133.3 81.8 %all-gather.6.cloned.1.call-start = ((), (), s32[]{:S(2)}) async-start(), calls=%async_computation.6 | async-start | bytes 5242880 | tf_op jit(solution)/shard_map/all_gather | solution.py:87
  215.1 4.8 %copy-start.1 = (bf16[256,8192]{1,0:T(8,128)(2,1)S(1)}, bf16[256,8192]{1,0:T(8,128)(2,1)}, u32[]{:S(2)}) copy-start(bf16[256,8192]{1,0:T(8,128)(2,1)} %all-gather.6.cloned.1.call-done) | copy-start | bytes 12582916
  219.9 35.2 %copy-start.2 = (bf16[8192,128]{1,0:T(8,128)(2,1)S(1)}, bf16[8192,128]{1,0:T(8,128)(2,1)}, u32[]{:S(2)}) copy-start(bf16[8192,128]{1,0:T(8,128)(2,1)} %param.15) | copy-start | bytes 6291460
Sparse Core Ops, SparseCore 0:
  9.8 26.1 all-gather.3
  92.2 33.6 reduce-scatter.1
  164.8 50.2 all-gather.5
where the time goes:
time: 305 us; the launch traced here: 304 us
  waiting for transfers between devices  118 us (39%)
  blocking collectives  114 us (37%)
  matrix products  24.7 us (8%)
  local copies, waits for them, and re-layouts  14.7 us (5%)
  between operations  14 us (5%)
  other arithmetic  11.2 us (4%)
  starting transfers between devices  7.98 us (3%)
    all_to_all x1, blocking collectives, body(): lax.all_to_all(strips, ('role', 'seq'), split_axis=0, concat_axis=1, tile...  51.7 us
    all_gather x1, waiting for transfers between devices, body(): shard_piece = lax.all_gather(normed, 'tp', axis=1, tiled=True)  49.5 us
    reduce_scatter x1, waiting for transfers between devices, sum_hidden(): lax.psum_scatter(partial_value, 'tp', scatter_dimension=1, tiled=True)  27.3 us
    all_gather x1, blocking collectives, body(): lax.all_gather(value_rows, ('role', 'seq'), axis=0, tiled=True)  26.6 us
    all_gather x1, blocking collectives, body(): key_piece = lax.all_gather(key_rows, ('role', 'seq'), axis=0, tiled=True)  26.5 us
    all_gather x1, waiting for transfers between devices, project_strips(): lax.all_gather(merger_hidden, ('role', 'seq'), axis=0, tiled=True)  26.2 us
    all_to_all x1, waiting for transfers between devices, body(): lax.all_to_all(outgoing, ('role', 'seq'), split_axis=0, concat_axis=0, ti...  14.6 us
    dot_general x3, matrix products, body(): jnp.dot(shard_piece, table, preferred_element_type=jnp.float32)  14.2 us
  transfers between devices with their start and end apart: 5, of which 4 were waited for; matrix products, arithmetic and copies ran while one was open for 2% of the time, Pallas kernels for 0%

commit v1 on v0

--- a/solution.py
+++ b/solution.py
@@ -84,7 +84,9 @@
     inverse = lax.rsqrt(squares / model_width + 1e-06)[:, None]
     normed = (widened * inverse * norm_gain.astype(jnp.float32)[None, :]).astype(jnp.bfloat16)
     tables = (query_weight, key_weight, value_weight)
-    shard_piece = lax.all_gather(normed, "tp", axis=1, tiled=True)
+    shard_piece = jnp.concatenate(
+        lax.all_to_all(jnp.stack([normed] * lax.axis_size("tp")), "tp", 0, 0), axis=1
+    )
     query_sum, key_sum, value_sum = tuple(
         (jnp.dot(shard_piece, table, preferred_element_type=jnp.float32) for table in tables)
     )

time: 305 us -> 317 us (1.039)
  local copies, waits for them, and re-layouts: 14.7 us -> 51.6 us
  waiting for transfers between devices: 118 us -> 94.8 us
  starting transfers between devices: 7.98 us -> 13 us
  other arithmetic: 11.2 us -> 7.34 us
  matrix products: 24.7 us -> 21.2 us
    all_gather x1 -> x0, waiting for transfers between devices: 49.5 us -> none  [body(): shard_piece = lax.all_gather(normed, 'tp', axis=1, tiled=True)]
    all_to_all x0 -> x1, waiting for transfers between devices: none -> 24.4 us  [body(): lax.all_to_all(jnp.stack([normed] * lax.axis_size('tp')), 'tp', 0, 0)]
    dot_general x0 -> x1, local copies, waits for them, and re-layouts: none -> 20.9 us  [body(): jnp.dot(shard_piece, table, preferred_element_type=jnp.float32)]
    reshape x0 -> x3, local copies, waits for them, and re-layouts: none -> 17.8 us  [body(): jnp.concatenate(lax.all_to_all(jnp.stack([normed] * lax.axis_size('tp')),...]
    all_to_all x0 -> x1, starting transfers between devices: none -> 5.04 us  [body(): lax.all_to_all(jnp.stack([normed] * lax.axis_size('tp')), 'tp', 0, 0)]
    dot_general x3, matrix products: 14.2 us -> 10.9 us  [body(): jnp.dot(shard_piece, table, preferred_element_type=jnp.float32)]
  transfers between devices with their start and end apart: 5 -> 5, of which waited for: 4 -> 4; matrix products, arithmetic and copies ran while one was open for 2% -> 9% of each run, Pallas kernels for 0% -> 0%
where the time goes in v1:
time: 317 us; the launch traced here: 316 us
  blocking collectives  113 us (36%)
  waiting for transfers between devices  94.8 us (30%)
  local copies, waits for them, and re-layouts  51.6 us (16%)
  matrix products  21.2 us (7%)
  between operations  14.3 us (5%)
  starting transfers between devices  13 us (4%)
  other arithmetic  7.34 us (2%)
    all_to_all x1, blocking collectives, body(): lax.all_to_all(strips, ('role', 'seq'), split_axis=0, concat_axis=1, tile...  51.7 us
    all_gather x1, waiting for transfers between devices, project_strips(): lax.all_gather(merger_hidden, ('role', 'seq'), axis=0, tiled=True)  27.8 us
    reduce_scatter x1, waiting for transfers between devices, sum_hidden(): lax.psum_scatter(partial_value, 'tp', scatter_dimension=1, tiled=True)  27.3 us
    all_gather x1, blocking collectives, body(): key_piece = lax.all_gather(key_rows, ('role', 'seq'), axis=0, tiled=True)  26.5 us
    all_gather x1, blocking collectives, body(): lax.all_gather(value_rows, ('role', 'seq'), axis=0, tiled=True)  26.2 us
    all_to_all x1, waiting for transfers between devices, body(): lax.all_to_all(jnp.stack([normed] * lax.axis_size('tp')), 'tp', 0, 0)  24.4 us
    dot_general x1, local copies, waits for them, and re-layouts, body(): jnp.dot(shard_piece, table, preferred_element_type=jnp.float32)  20.9 us
    reshape x3, local copies, waits for them, and re-layouts, body(): jnp.concatenate(lax.all_to_all(jnp.stack([normed] * lax.axis_size('tp')),...  17.8 us
  transfers between devices with their start and end apart: 5, of which 4 were waited for; matrix products, arithmetic and copies ran while one was open for 9% of the time, Pallas kernels for 0%

profile of v1, /device:TPU:0, one launch (start us, length us, event | category | flops | bytes accessed | tf_op | source)
XLA Modules:
  0.0 315.6 jit_solution(14108725457278853738)
XLA Ops:
  8.0 27.8 %all-gather.3.cloned.1.call-done = bf16[512,1280]{1,0:T(8,128)(2,1)} async-done(((bf16[64,1280]{1,0:T(8,128)(2,1)}), bf16[512,1280]{1,0:T(8,128)(2,1)}) %all-gather.3.cloned.1.call-update) | async-done | bytes 1310736 | tf_op jit(solution)/shard_map/all_gather | solution.py:35
  35.7 2.8 fusion.36
  38.6 51.7 %all_to_all.38 = f32[8,64,1024]{2,1,0:T(8,128)S(1)} all-to-all(f32[8,64,1024]{2,1,0:T(8,128)S(1)} %bitcast.70), channel_id=1, replica_groups=mesh['role'=2,'seq'=4,'tp'=4] {'role','seq'}, dimensions={0} | all-to-all | bytes 4194304 | tf_op jit(solution)/shard_map/all_to_all | solution.py:59
  95.0 3.3 %all-to-all-start = ((s32[8,1,16]{2,1,0:T(1,128)}), s32[8,1,16]{2,1,0:T(1,128)S(1)}, u32[]{:S(2)}, u32[]{:S(2)}) async-start(s32[8,1,16]{2,1,0:T(1,128)} %bitcast), calls=%async_computation | async-start | bytes 8192 | tf_op jit(solution)/shard_map/all_to_all | solution.py:77
  98.3 27.3 %reduce-scatter.2.cloned.1.call-done = f32[64,2048]{1,0:T(8,128)} async-done(((f32[64,8192]{1,0:T(8,128)}), f32[64,2048]{1,0:T(8,128)}) %reduce-scatter.2.cloned.1.call-update) | async-done | bytes 524304 | tf_op jit(solution)/shard_map/reduce_scatter | solution.py:28
  126.7 1.7 gather_fusion.1
  128.4 4.6 %all-to-all-start.2 = ((bf16[8,16,2048]{2,1,0:T(8,128)(2,1)}), bf16[8,16,2048]{2,1,0:T(8,128)(2,1)S(1)}, u32[]{:S(2)}, u32[]{:S(2)}) async-start(bf16[8,16,2048]{2,1,0:T(8,128)(2,1)} %bitcast.4), calls=%async_computation.3 | async-start | bytes 1048576 | tf_op jit(solution)/shard_map/all_to_all | solution.py:76
  133.2 14.6 %all-to-all-done.2 = bf16[8,16,2048]{2,1,0:T(8,128)(2,1)S(1)} async-done(((bf16[8,16,2048]{2,1,0:T(8,128)(2,1)}), bf16[8,16,2048]{2,1,0:T(8,128)(2,1)S(1)}, u32[]{:S(2)}, u32[]{:S(2)}) %all-to-all-start.2) | async-done | bytes 524320 | tf_op jit(solution)/shard_map/all_to_all | solution.py:76
  147.8 1.9 scatter_fusion
  150.0 8.9 %psum.7 = f32[256]{0:T(256)S(1)} all-reduce(f32[256]{0:T(256)S(1)} %fusion.7), channel_id=1, replica_groups=mesh['role'=2,'seq'=4,'tp'=4] {'tp'}, use_global_device_ids=true, to_apply=%region_6.7 | all-reduce | flops 256 | bytes 2048 | tf_op jit(solution)/shard_map/psum | solution.py:83
  159.3 2.5 stack.2
  161.8 5.0 %all-to-all-start.3 = ((bf16[4,256,2048]{2,1,0:T(8,128)(2,1)}), bf16[4,256,2048]{2,1,0:T(8,128)(2,1)}, u32[]{:S(2)}, u32[]{:S(2)}) async-start(bf16[4,256,2048]{2,1,0:T(8,128)(2,1)} %stack.2), calls=%async_computation.4 | async-start | bytes 8388608 | tf_op jit(solution)/shard_map/all_to_all | solution.py:88
  166.9 20.9 %copy.36 = bf16[1024,8192]{1,0:T(8,128)(2,1)} copy(bf16[1024,8192]{0,1:T(8,128)(2,1)} %bitcast.65) | data formatting | bytes 33554432 | tf_op jit(solution)/shard_map/dot_general | solution.py:91
  188.5 24.4 %all-to-all-done.3 = bf16[4,256,2048]{2,1,0:T(8,128)(2,1)} async-done(((bf16[4,256,2048]{2,1,0:T(8,128)(2,1)}), bf16[4,256,2048]{2,1,0:T(8,128)(2,1)}, u32[]{:S(2)}, u32[]{:S(2)}) %all-to-all-start.3) | async-done | bytes 4194336 | tf_op jit(solution)/shard_map/all_to_all | solution.py:88
  212.9 7.4 %copy.24 = bf16[256,4,2048]{2,1,0:T(4,128)(2,1)} copy(bf16[256,4,2048]{2,0,1:T(8,128)(2,1)} %bitcast.6) | data formatting | bytes 8388608 | tf_op jit(solution)/shard_map/reshape | solution.py:87
  220.3 7.8 %reshape.307 = bf16[256,8192,1]{1,0,2:T(8,128)(2,1)} reshape(bf16[256,4,2048]{2,1,0:T(4,128)(2,1)} %copy.24) | data formatting | bytes 8388608 | tf_op jit(solution)/shard_map/reshape | solution.py:87
  228.1 2.6 copy.39
  234.2 26.5 %all_gather.10 = bf16[2048,1,128]{0,2,1:T(8,128)(2,1)S(1)} all-gather(bf16[256,1,128]{0,2,1:T(8,128)(2,1)S(1)} %pad_maximum_fusion), channel_id=1, replica_groups=mesh['role'=2,'seq'=4,'tp'=4] {'role','seq'}, dimensions={0}, use_global_device_ids=true | all-gather | bytes 589824 | tf_op jit(solution)/shard_map/all_gather | solution.py:107
  260.7 26.2 %all-gather = bf16[2048,128]{1,0:T(8,128)(2,1)S(1)} all-gather(bf16[256,128]{1,0:T(8,128)(2,1)S(1)} %convolution_convert_fusion), channel_id=2, replica_groups=mesh['role'=2,'seq'=4,'tp'=4] {'role','seq'}, dimensions={0}, use_global_device_ids=true | all-gather | bytes 589824 | tf_op jit(solution)/shard_map/all_gather | solution.py:108
  286.9 8.2 %fusion.37 = f32[256,8,128]{0,2,1:T(8,128)S(1)} fusion(bf16[256,8192,1]{1,0,2:T(8,128)(2,1)S(1)} %copy-done.4, bf16[8,128,8192]{2,1,0:T(8,128)(2,1)} %bitcast.66), kind=kOutput, calls=%fused_computation.71 | convolution fusion | flops 4294967296 | bytes 22020096 | tf_op jit(solution)/shard_map/dot_general | solution.py:91
  295.2 2.6 fusion
  297.8 4.0 %fusion.1 = f32[8,256]{1,0:T(8,128)S(1)} fusion(f32[2048,256,8]{1,0,2:T(8,128)S(1)} %get-tuple-element.15, f32[8,256]{1,0:T(8,128)S(1)} %broadcast_maximum_fusion, pred[256,2048]{0,1:T(8,128)(4,1)S(1)} %iota_compare_fusion), kind=kLoop, calls=%fused_computation.7 | loop fusion | flops 20969472 | bytes 17317888 | tf_op jit(solution)/shard_map/reduce_sum | solution.py:118
  301.8 4.9 %divide_convert_fusion = bf16[8,256,128]{1,2,0:T(8,128)(2,1)} fusion(f32[2048,256,8]{1,0,2:T(8,128)S(1)} %get-tuple-element.15, f32[8,256]{1,0:T(8,128)S(1)} %broadcast_maximum_fusion, pred[256,2048]{0,1:T(8,128)(4,1)S(1)} %iota_compare_fusion, bf16[2048,128]{1,0:T(8,128)(2,1)S(1)} %all-gather, f32[8,256]{1,0:T(8,128)S(1)} %fusion.1), kind=kOutput, calls=%fused_computation.20 | convolution fusion | flops 1095237632 | bytes 18366464 | tf_op jit(solution)/shard_map/hgqk,khd->hgqd/dot_general | solution.py:119
  306.7 2.0 copy.30
  (56 shorter events, 11.6 us)
Async XLA Ops:
  7.2 28.6 %copy-start = (bf16[1280,1024]{1,0:T(8,128)(2,1)S(1)}, bf16[1280,1024]{1,0:T(8,128)(2,1)}, u32[]{:S(2)}) copy-start(bf16[1280,1024]{1,0:T(8,128)(2,1)} %param.9) | copy-start | bytes 7864324
  7.2 28.6 %all-gather.3.cloned.1.call-start = ((), (), s32[]{:S(2)}) async-start(), calls=%async_computation.5 | async-start | bytes 1474560 | tf_op jit(solution)/shard_map/all_gather | solution.py:35
  7.9 117.7 %reduce-scatter.2.cloned.1.call-start = ((), (), s32[]{:S(2)}) async-start(), calls=%async_computation.6 | async-start | bytes 2621440 | tf_op jit(solution)/shard_map/reduce_scatter | solution.py:28
  90.3 1.5 copy-start.8
  91.8 41.2 %copy-start.7 = (bf16[2048]{0:T(1024)(128)(2,1)S(1)}, bf16[2048]{0:T(1024)(128)(2,1)}, u32[]{:S(2)}) copy-start(bf16[2048]{0:T(1024)(128)(2,1)} %param.12) | copy-start | bytes 12292
  91.8 56.0 %copy-start.3 = (bf16[256,2048]{1,0:T(8,128)(2,1)S(1)}, bf16[256,2048]{1,0:T(8,128)(2,1)}, u32[]{:S(2)}) copy-start(bf16[256,2048]{1,0:T(8,128)(2,1)} %param.11) | copy-start | bytes 3145732
  95.0 33.4 %all-to-all-start = ((s32[8,1,16]{2,1,0:T(1,128)}), s32[8,1,16]{2,1,0:T(1,128)S(1)}, u32[]{:S(2)}, u32[]{:S(2)}) async-start(s32[8,1,16]{2,1,0:T(1,128)} %bitcast), calls=%async_computation | async-start | bytes 8192 | tf_op jit(solution)/shard_map/all_to_all | solution.py:77
  128.4 19.4 %all-to-all-start.2 = ((bf16[8,16,2048]{2,1,0:T(8,128)(2,1)}), bf16[8,16,2048]{2,1,0:T(8,128)(2,1)S(1)}, u32[]{:S(2)}, u32[]{:S(2)}) async-start(bf16[8,16,2048]{2,1,0:T(8,128)(2,1)} %bitcast.4), calls=%async_computation.3 | async-start | bytes 1048576 | tf_op jit(solution)/shard_map/all_to_all | solution.py:76
  149.7 12.1 %copy-start.2 = (bf16[256,2048]{1,0:T(8,128)(2,1)}, bf16[256,2048]{1,0:T(8,128)(2,1)S(1)}, u32[]{:S(2)}) copy-start(bf16[256,2048]{1,0:T(8,128)(2,1)S(1)} %scatter_fusion) | copy-start | bytes 3145732
  161.8 51.1 %all-to-all-start.3 = ((bf16[4,256,2048]{2,1,0:T(8,128)(2,1)}), bf16[4,256,2048]{2,1,0:T(8,128)(2,1)}, u32[]{:S(2)}, u32[]{:S(2)}) async-start(bf16[4,256,2048]{2,1,0:T(8,128)(2,1)} %stack.2), calls=%async_computation.4 | async-start | bytes 8388608 | tf_op jit(solution)/shard_map/all_to_all | solution.py:88
  228.1 2.9 copy-start.5
  230.7 1.6 copy-start.6
  232.3 54.5 %copy-start.4 = (bf16[256,8192,1]{1,0,2:T(8,128)(2,1)S(1)}, bf16[256,8192,1]{1,0,2:T(8,128)(2,1)}, u32[]{:S(2)}) copy-start(bf16[256,8192,1]{1,0,2:T(8,128)(2,1)} %reshape.307) | copy-start | bytes 12582916
  301.8 6.9 %copy-start.1 = (bf16[1280,1024]{1,0:T(8,128)(2,1)S(1)}, bf16[1280,1024]{1,0:T(8,128)(2,1)}, u32[]{:S(2)}) copy-start(bf16[1280,1024]{1,0:T(8,128)(2,1)} %param.9) | copy-start | bytes 7864324
Sparse Core Ops, SparseCore 0:
  9.6 26.1 all-gather.2
  91.9 33.6 reduce-scatter.1
